TPU v7x, 512 devices: a whole 4x4x16 slice. The times are simulated.
512 devices in a mesh: grp: 8 (over x, core), wide: 64 (over z, y).
Axes of the slice: x: 4, y: 4, z: 16, core: 2. Of those that a mesh axis runs over, the one named last changes fastest.
Arguments:
- anchor_states: bfloat16 [65536, 1024], P(('wide', 'grp')), may hold values from -6 to 6
- key_weight: bfloat16 [1024, 1024], P(None, 'grp'), may hold values from -0.1875 to 0.1875
- value_weight: bfloat16 [1024, 1024], P(None, 'grp'), may hold values from -0.1875 to 0.1875
- panel_query: bfloat16 [131072, 1024], P(('wide', 'grp')), may hold values from -160 to 160
- cell_list: int32 [1024, 4], P('wide'), may hold values from 0 to 7, as said below
- cell_count: int32 [1024], P('wide'), may hold values from 1 to 4, as said below
- norm_gain: float32 [1024], replicated, may hold values from 0.1 to 1.9
- up_weight: bfloat16 [1024, 512], replicated, may hold values from -0.1875 to 0.1875
- flux_weight: bfloat16 [4, 512], replicated, may hold values from -0.25 to 0.25
Outputs:
- flux: float32 [4, 131072], P(None, ('wide', 'grp'))
Inputs may be any that keep to these rules, and one draw needn't show every extreme that they name: `cell_list`: the entries of a row are distinct cell blocks of that panel block's region; entries past cell_count are not used. `cell_count`: every region has a panel block whose list uses all 4 slots.
All inputs are finite; a program needn't handle non-finite values.
Results may differ from a plain program's by a relative error of at most 0.007.
Values may be sent and summed in bfloat16 or wider, within the bound.
No kernel may reach another device: no remote copies, remote signals or barrier semaphores. Data moves between devices by JAX's collectives and lax.ppermute only.
A program may use at most 64 MiB of HBM per device.

v0:
```python
import math
import jax
import jax.numpy as jnp
from jax import lax
from jax.sharding import PartitionSpec as P

BLK = 128
LMAX = 4
HD = 64


def softmax_rows(scores, mask):
    scores = jnp.where(mask[:, None, None, :], scores, -jnp.inf)
    top = jnp.max(scores, axis=-1, keepdims=True)
    expo = jnp.exp(scores - top)
    return (expo / jnp.sum(expo, axis=-1, keepdims=True)).astype(jnp.bfloat16)


def wall_flux(query_rows, attended_rows, norm_gain, up_weight, flux_weight):
    stream = query_rows.astype(jnp.float32) + attended_rows.astype(jnp.float32)
    scale = lax.rsqrt(jnp.mean(stream * stream, axis=-1, keepdims=True) + 1e-06)
    normed = (stream * scale * norm_gain[None, :]).astype(jnp.bfloat16)
    hidden = jax.nn.gelu(jnp.dot(normed, up_weight, preferred_element_type=jnp.float32)).astype(
        jnp.bfloat16
    )
    return lax.dot_general(
        flux_weight, hidden, (((1,), (1,)), ((), ())), preferred_element_type=jnp.float32
    )


def body(
    anchor_states,
    key_weight,
    value_weight,
    panel_query,
    cell_list,
    cell_count,
    norm_gain,
    up_weight,
    flux_weight,
):
    full_keys_w, full_values_w = (
        lax.all_gather(key_weight, "grp", axis=1, tiled=True),
        lax.all_gather(value_weight, "grp", axis=1, tiled=True),
    )
    local_keys = jnp.dot(anchor_states, full_keys_w, preferred_element_type=jnp.float32).astype(
        jnp.bfloat16
    )
    local_values = jnp.dot(anchor_states, full_values_w, preferred_element_type=jnp.float32).astype(
        jnp.bfloat16
    )
    region_keys, region_values = (
        lax.all_to_all(local_keys, "grp", split_axis=1, concat_axis=0, tiled=True),
        lax.all_to_all(local_values, "grp", split_axis=1, concat_axis=0, tiled=True),
    )
    region_query = lax.all_to_all(
        lax.all_to_all(panel_query, "grp", split_axis=1, concat_axis=0, tiled=True),
        "wide",
        split_axis=0,
        concat_axis=0,
        tiled=True,
    )
    local_heads = region_keys.shape[1] // HD
    cell_blocks = region_keys.shape[0] // BLK
    block_count = region_query.shape[0] // BLK
    per_step = math.gcd(block_count, 4)
    steps = block_count // per_step
    key_blocks = region_keys.reshape(cell_blocks, BLK, local_heads, HD)
    value_blocks = region_values.reshape(cell_blocks, BLK, local_heads, HD)
    query_groups = region_query.reshape(steps, per_step, BLK, local_heads, HD)
    list_groups = cell_list.reshape(steps, per_step, LMAX)
    count_groups = cell_count.reshape(steps, per_step)
    slot_index = jnp.arange(LMAX, dtype=jnp.int32)

    def attend(item):
        query_group, listed, counts = item
        live = slot_index[None, :] < counts[:, None]
        picked_keys = key_blocks[listed].reshape(per_step, LMAX * BLK, local_heads, HD)
        picked_values = value_blocks[listed].reshape(per_step, LMAX * BLK, local_heads, HD)
        mask = jnp.repeat(live, BLK, axis=1)
        scores = jnp.einsum(
            "bihd,bjhd->bhij", query_group, picked_keys, preferred_element_type=jnp.float32
        ) / math.sqrt(HD)
        weights = softmax_rows(scores, mask)
        output = jnp.einsum(
            "bhij,bjhd->bihd", weights, picked_values, preferred_element_type=jnp.float32
        )
        return output.astype(jnp.bfloat16)

    attended = lax.map(attend, (query_groups, list_groups, count_groups))
    attended = attended.reshape(block_count * BLK, local_heads * HD)
    panel_rows = lax.all_to_all(
        lax.all_to_all(attended, "wide", split_axis=0, concat_axis=0, tiled=True),
        "grp",
        split_axis=0,
        concat_axis=1,
        tiled=True,
    )
    return wall_flux(panel_query, panel_rows, norm_gain, up_weight, flux_weight)


def solution(mesh):
    in_specs = (
        P(("wide", "grp"), None),
        P(None, "grp"),
        P(None, "grp"),
        P(("wide", "grp"), None),
        P("wide", None),
        P("wide"),
        P(),
        P(),
        P(),
    )
    out_specs = P(None, ("wide", "grp"))
    return jax.shard_map(body, mesh=mesh, in_specs=in_specs, out_specs=out_specs, check_vma=False)
```

profile of v0, /device:TPU:1, one launch (start us, length us, event | category | flops | bytes accessed | tf_op | source)
XLA Modules:
  0.0 225.5 jit_solution(5993352546024872910)
XLA Ops:
  9.3 18.6 %all_to_all.79 = bf16[256,8,128]{0,2,1:T(8,128)(2,1)S(1)} all-to-all(bf16[256,8,128]{0,2,1:T(8,128)(2,1)S(1)} %bitcast.78), channel_id=1, replica_groups=mesh['grp'=8,'wide'=64] {'grp'}, dimensions={1} | all-to-all | bytes 1048576 | tf_op jit(solution)/shard_map/all_to_all | solution.py:57
  29.0 14.8 %all-to-all-start.2 = ((bf16[64,32,128]{2,1,0:T(8,128)(2,1)}), bf16[64,32,128]{2,1,0:T(8,128)(2,1)S(1)}, u32[]{:S(2)}, u32[]{:S(2)}) async-start(bf16[64,32,128]{2,1,0:T(8,128)(2,1)} %bitcast.6), calls=%async_computation.2 | async-start | bytes 1048576 | tf_op jit(solution)/shard_map/all_to_all | solution.py:56
  43.7 6.4 %all-gather.3.cloned.1.call-done = bf16[1024,1024]{1,0:T(8,128)(2,1)} async-done(((bf16[1024,128]{1,0:T(8,128)(2,1)}), bf16[1024,1024]{1,0:T(8,128)(2,1)}) %all-gather.3.cloned.1.call-update) | async-done | bytes 2097168 | tf_op jit(solution)/shard_map/all_gather | solution.py:44
  50.1 2.0 convolution_convert_fusion.2
  53.0 19.9 %all-to-all-done.2 = bf16[64,32,128]{2,1,0:T(8,128)(2,1)S(1)} async-done(((bf16[64,32,128]{2,1,0:T(8,128)(2,1)}), bf16[64,32,128]{2,1,0:T(8,128)(2,1)S(1)}, u32[]{:S(2)}, u32[]{:S(2)}) %all-to-all-start.2) | async-done | bytes 524320 | tf_op jit(solution)/shard_map/all_to_all | solution.py:56
  72.9 8.1 %all-to-all-start = ((bf16[128,8,128]{0,2,1:T(8,128)(2,1)}), bf16[128,8,128]{0,2,1:T(8,128)(2,1)S(1)}, u32[]{:S(2)}, u32[]{:S(2)}) async-start(bf16[128,8,128]{0,2,1:T(8,128)(2,1)} %bitcast.1), calls=%async_computation | async-start | bytes 524288 | tf_op jit(solution)/shard_map/all_to_all | solution.py:54
  81.0 10.1 %all-gather.5.cloned.1.call-done = bf16[1024,1024]{1,0:T(8,128)(2,1)} async-done(((bf16[1024,128]{1,0:T(8,128)(2,1)}), bf16[1024,1024]{1,0:T(8,128)(2,1)}) %all-gather.5.cloned.1.call-update) | async-done | bytes 2097168 | tf_op jit(solution)/shard_map/all_gather | solution.py:43
  91.1 2.0 convolution_convert_fusion.1
  93.9 4.2 %all-to-all-start.3 = ((bf16[128,8,128]{0,2,1:T(8,128)(2,1)}), bf16[128,8,128]{0,2,1:T(8,128)(2,1)S(1)}, u32[]{:S(2)}, u32[]{:S(2)}) async-start(bf16[128,8,128]{0,2,1:T(8,128)(2,1)} %bitcast.7), calls=%async_computation.3 | async-start | bytes 524288 | tf_op jit(solution)/shard_map/all_to_all | solution.py:53
  98.8 1.8 copy.33
  100.9 3.8 %all-to-all-done.3 = bf16[128,8,128]{0,2,1:T(8,128)(2,1)S(1)} async-done(((bf16[128,8,128]{0,2,1:T(8,128)(2,1)}), bf16[128,8,128]{0,2,1:T(8,128)(2,1)S(1)}, u32[]{:S(2)}, u32[]{:S(2)}) %all-to-all-start.3) | async-done | bytes 262176 | tf_op jit(solution)/shard_map/all_to_all | solution.py:53
  105.1 46.4 %while.11 = (s32[]{:T(128)}, bf16[4,4,128,2,64]{2,4,3,1,0:T(8,128)(2,1)}, s32[4,4,4]{2,1,0:T(4,128)S(1)}, bf16[8,128,2,64]{3,2,1,0:T(2,128)(2,1)S(1)}, s32[4,4]{...) while((s32[]{:T(128)}, ...), condition=%wide.region_3.4_spmd.clone, body=%wide.region_0.3_spmd.clone.sunk | while | flops 137430592 | bytes 7624301 | solution.py:90
  105.2 2.7 %gather_fusion.1 = bf16[16,128,2,64]{3,2,1,0:T(2,128)(2,1)S(1)} fusion(bf16[8,128,2,64]{3,2,1,0:T(2,128)(2,1)S(1)} %get-tuple-element.170, s32[1024]{0:T(1024)S(1)} %pad_clamp_fusion.2), kind=kCustom, calls=%fused_computation.1.clone.clone.1 | custom fusion | bytes 1048640 | tf_op jit(solution)/shard_map/while/body/eval_jaxpr/gather | solution.py:78
  108.1 3.1 %fusion.69 = (f32[4,2,128]{2,1,0:T(2,128)S(1)}, f32[4,2,128,512]{3,2,1,0:T(8,128)}) fusion(pred[4,512]{1,0:T(4,128)(4,1)S(1)} %bitcast.83, bf16[4,512,2,64]{3,2,1,0:T(2,128)(2,1)S(1)} %bitcast.76, bf16[4,4,128,2,64]{2,4,3,1,0:T(8,128)(2,1)} %get-tuple-element.169, s32[]{:T(128)} %get-tuple-element.156), kind=kOutput, calls=%fused_computation.51.clone.1 | convolution fusion | flops 69206528 | bytes 2759168 | tf_op jit(solution)/shard_map/while/body/eval_jaxpr/sub | solution.py:15
  111.1 2.7 %gather_fusion = bf16[16,128,2,64]{3,2,1,0:T(2,128)(2,1)S(1)} fusion(bf16[8,128,2,64]{3,2,1,0:T(2,128)(2,1)S(1)} %get-tuple-element.167, s32[1024]{0:T(1024)S(1)} %pad_clamp_fusion.2), kind=kCustom, calls=%fused_computation.clone.clone.1 | custom fusion | bytes 1048640 | tf_op jit(solution)/shard_map/while/body/eval_jaxpr/gather | solution.py:79
  113.8 2.9 %fusion.70 = bf16[4,4,128,2,64]{2,4,3,1,0:T(8,128)(2,1)} fusion(bf16[4,4,128,2,64]{2,4,3,1,0:T(8,128)(2,1)} %get-tuple-element.157, s32[]{:T(128)} %get-tuple-element.156, bf16[4,512,2,64]{3,2,1,0:T(2,128)(2,1)S(1)} %bitcast.77, f32[4,2,128,512]{3,2,1,0:T(8,128)} %get-tuple-element.146, f32[4,2,128]{2,1,0:T(2,128)S(1)} %get-tuple-element.147), kind=kOutput, calls=%fused_computation.10.clone.1 | convolution fusion | flops 68222976 | bytes 2757120 | tf_op jit(solution)/shard_map/while/body/eval_jaxpr/bhij,bjhd->bihd/dot_general | solution.py:85
  116.8 2.7 %gather_fusion.1 = bf16[16,128,2,64]{3,2,1,0:T(2,128)(2,1)S(1)} fusion(bf16[8,128,2,64]{3,2,1,0:T(2,128)(2,1)S(1)} %get-tuple-element.170, s32[1024]{0:T(1024)S(1)} %pad_clamp_fusion.2), kind=kCustom, calls=%fused_computation.1.clone.clone.1 | custom fusion | bytes 1048640 | tf_op jit(solution)/shard_map/while/body/eval_jaxpr/gather | solution.py:78
  119.6 3.1 %fusion.69 = (f32[4,2,128]{2,1,0:T(2,128)S(1)}, f32[4,2,128,512]{3,2,1,0:T(8,128)}) fusion(pred[4,512]{1,0:T(4,128)(4,1)S(1)} %bitcast.83, bf16[4,512,2,64]{3,2,1,0:T(2,128)(2,1)S(1)} %bitcast.76, bf16[4,4,128,2,64]{2,4,3,1,0:T(8,128)(2,1)} %get-tuple-element.169, s32[]{:T(128)} %get-tuple-element.156), kind=kOutput, calls=%fused_computation.51.clone.1 | convolution fusion | flops 69206528 | bytes 2759168 | tf_op jit(solution)/shard_map/while/body/eval_jaxpr/sub | solution.py:15
  122.7 2.7 %gather_fusion = bf16[16,128,2,64]{3,2,1,0:T(2,128)(2,1)S(1)} fusion(bf16[8,128,2,64]{3,2,1,0:T(2,128)(2,1)S(1)} %get-tuple-element.167, s32[1024]{0:T(1024)S(1)} %pad_clamp_fusion.2), kind=kCustom, calls=%fused_computation.clone.clone.1 | custom fusion | bytes 1048640 | tf_op jit(solution)/shard_map/while/body/eval_jaxpr/gather | solution.py:79
  125.4 2.9 %fusion.70 = bf16[4,4,128,2,64]{2,4,3,1,0:T(8,128)(2,1)} fusion(bf16[4,4,128,2,64]{2,4,3,1,0:T(8,128)(2,1)} %get-tuple-element.157, s32[]{:T(128)} %get-tuple-element.156, bf16[4,512,2,64]{3,2,1,0:T(2,128)(2,1)S(1)} %bitcast.77, f32[4,2,128,512]{3,2,1,0:T(8,128)} %get-tuple-element.146, f32[4,2,128]{2,1,0:T(2,128)S(1)} %get-tuple-element.147), kind=kOutput, calls=%fused_computation.10.clone.1 | convolution fusion | flops 68222976 | bytes 2757120 | tf_op jit(solution)/shard_map/while/body/eval_jaxpr/bhij,bjhd->bihd/dot_general | solution.py:85
  128.4 2.7 %gather_fusion.1 = bf16[16,128,2,64]{3,2,1,0:T(2,128)(2,1)S(1)} fusion(bf16[8,128,2,64]{3,2,1,0:T(2,128)(2,1)S(1)} %get-tuple-element.170, s32[1024]{0:T(1024)S(1)} %pad_clamp_fusion.2), kind=kCustom, calls=%fused_computation.1.clone.clone.1 | custom fusion | bytes 1048640 | tf_op jit(solution)/shard_map/while/body/eval_jaxpr/gather | solution.py:78
  131.2 3.1 %fusion.69 = (f32[4,2,128]{2,1,0:T(2,128)S(1)}, f32[4,2,128,512]{3,2,1,0:T(8,128)}) fusion(pred[4,512]{1,0:T(4,128)(4,1)S(1)} %bitcast.83, bf16[4,512,2,64]{3,2,1,0:T(2,128)(2,1)S(1)} %bitcast.76, bf16[4,4,128,2,64]{2,4,3,1,0:T(8,128)(2,1)} %get-tuple-element.169, s32[]{:T(128)} %get-tuple-element.156), kind=kOutput, calls=%fused_computation.51.clone.1 | convolution fusion | flops 69206528 | bytes 2759168 | tf_op jit(solution)/shard_map/while/body/eval_jaxpr/sub | solution.py:15
  134.3 2.7 %gather_fusion = bf16[16,128,2,64]{3,2,1,0:T(2,128)(2,1)S(1)} fusion(bf16[8,128,2,64]{3,2,1,0:T(2,128)(2,1)S(1)} %get-tuple-element.167, s32[1024]{0:T(1024)S(1)} %pad_clamp_fusion.2), kind=kCustom, calls=%fused_computation.clone.clone.1 | custom fusion | bytes 1048640 | tf_op jit(solution)/shard_map/while/body/eval_jaxpr/gather | solution.py:79
  137.0 2.9 %fusion.70 = bf16[4,4,128,2,64]{2,4,3,1,0:T(8,128)(2,1)} fusion(bf16[4,4,128,2,64]{2,4,3,1,0:T(8,128)(2,1)} %get-tuple-element.157, s32[]{:T(128)} %get-tuple-element.156, bf16[4,512,2,64]{3,2,1,0:T(2,128)(2,1)S(1)} %bitcast.77, f32[4,2,128,512]{3,2,1,0:T(8,128)} %get-tuple-element.146, f32[4,2,128]{2,1,0:T(2,128)S(1)} %get-tuple-element.147), kind=kOutput, calls=%fused_computation.10.clone.1 | convolution fusion | flops 68222976 | bytes 2757120 | tf_op jit(solution)/shard_map/while/body/eval_jaxpr/bhij,bjhd->bihd/dot_general | solution.py:85
  140.0 2.7 %gather_fusion.1 = bf16[16,128,2,64]{3,2,1,0:T(2,128)(2,1)S(1)} fusion(bf16[8,128,2,64]{3,2,1,0:T(2,128)(2,1)S(1)} %get-tuple-element.170, s32[1024]{0:T(1024)S(1)} %pad_clamp_fusion.2), kind=kCustom, calls=%fused_computation.1.clone.clone.1 | custom fusion | bytes 1048640 | tf_op jit(solution)/shard_map/while/body/eval_jaxpr/gather | solution.py:78
  142.8 3.1 %fusion.69 = (f32[4,2,128]{2,1,0:T(2,128)S(1)}, f32[4,2,128,512]{3,2,1,0:T(8,128)}) fusion(pred[4,512]{1,0:T(4,128)(4,1)S(1)} %bitcast.83, bf16[4,512,2,64]{3,2,1,0:T(2,128)(2,1)S(1)} %bitcast.76, bf16[4,4,128,2,64]{2,4,3,1,0:T(8,128)(2,1)} %get-tuple-element.169, s32[]{:T(128)} %get-tuple-element.156), kind=kOutput, calls=%fused_computation.51.clone.1 | convolution fusion | flops 69206528 | bytes 2759168 | tf_op jit(solution)/shard_map/while/body/eval_jaxpr/sub | solution.py:15
  145.9 2.7 %gather_fusion = bf16[16,128,2,64]{3,2,1,0:T(2,128)(2,1)S(1)} fusion(bf16[8,128,2,64]{3,2,1,0:T(2,128)(2,1)S(1)} %get-tuple-element.167, s32[1024]{0:T(1024)S(1)} %pad_clamp_fusion.2), kind=kCustom, calls=%fused_computation.clone.clone.1 | custom fusion | bytes 1048640 | tf_op jit(solution)/shard_map/while/body/eval_jaxpr/gather | solution.py:79
  148.6 2.9 %fusion.70 = bf16[4,4,128,2,64]{2,4,3,1,0:T(8,128)(2,1)} fusion(bf16[4,4,128,2,64]{2,4,3,1,0:T(8,128)(2,1)} %get-tuple-element.157, s32[]{:T(128)} %get-tuple-element.156, bf16[4,512,2,64]{3,2,1,0:T(2,128)(2,1)S(1)} %bitcast.77, f32[4,2,128,512]{3,2,1,0:T(8,128)} %get-tuple-element.146, f32[4,2,128]{2,1,0:T(2,128)S(1)} %get-tuple-element.147), kind=kOutput, calls=%fused_computation.10.clone.1 | convolution fusion | flops 68222976 | bytes 2757120 | tf_op jit(solution)/shard_map/while/body/eval_jaxpr/bhij,bjhd->bihd/dot_general | solution.py:85
  151.5 2.4 %copy.35 = bf16[4,4,128,2,64]{4,3,2,1,0:T(2,128)(2,1)S(1)} copy(bf16[4,4,128,2,64]{2,4,3,1,0:T(8,128)(2,1)} %get-tuple-element.47) | data formatting | bytes 1048576 | tf_op jit(solution)/shard_map/while | solution.py:90
  154.3 43.2 %all_to_all.80 = bf16[64,32,128]{2,1,0:T(8,128)(2,1)S(1)} all-to-all(bf16[64,32,128]{2,1,0:T(8,128)(2,1)S(1)} %all_to_all.69), channel_id=1, replica_groups=mesh['grp'=8,'wide'=64] {'wide'}, dimensions={0} | all-to-all | bytes 1048576 | tf_op jit(solution)/shard_map/all_to_all | solution.py:93
  197.6 16.5 %all_to_all.81 = bf16[8,256,128]{2,1,0:T(8,128)(2,1)S(1)} all-to-all(bf16[8,256,128]{2,1,0:T(8,128)(2,1)S(1)} %bitcast.79), channel_id=1, replica_groups=mesh['grp'=8,'wide'=64] {'grp'}, dimensions={0} | all-to-all | bytes 1048576 | tf_op jit(solution)/shard_map/all_to_all | solution.py:92
  215.1 1.6 copy.36
  (65 shorter events, 11.3 us)
Async XLA Ops:
  6.5 210.6 %copy-start = (bf16[1024,512]{1,0:T(8,128)(2,1)S(1)}, bf16[1024,512]{1,0:T(8,128)(2,1)}, u32[]{:S(2)}) copy-start(bf16[1024,512]{1,0:T(8,128)(2,1)} %param.18) | copy-start | bytes 3145732
  6.5 43.6 %all-gather.3.cloned.1.call-start = ((), (), s32[]{:S(2)}) async-start(), calls=%async_computation.6 | async-start | bytes 2359296 | tf_op jit(solution)/shard_map/all_gather | solution.py:44
  7.3 83.8 %all-gather.5.cloned.1.call-start = ((), (), s32[]{:S(2)}) async-start(), calls=%async_computation.7 | async-start | bytes 2359296 | tf_op jit(solution)/shard_map/all_gather | solution.py:43
  8.0 42.1 %copy-start.3 = (bf16[128,1024]{1,0:T(8,128)(2,1)S(1)}, bf16[128,1024]{1,0:T(8,128)(2,1)}, u32[]{:S(2)}) copy-start(bf16[128,1024]{1,0:T(8,128)(2,1)} %param.11) | copy-start | bytes 786436
  9.3 42.9 %copy-start.1 = (bf16[256,1024]{0,1:T(8,128)(2,1)}, bf16[256,1024]{0,1:T(8,128)(2,1)S(1)}, u32[]{:S(2)}) copy-start(bf16[256,1024]{0,1:T(8,128)(2,1)S(1)} %copy.26) | copy-start | bytes 1572868
  29.0 43.9 %all-to-all-start.2 = ((bf16[64,32,128]{2,1,0:T(8,128)(2,1)}), bf16[64,32,128]{2,1,0:T(8,128)(2,1)S(1)}, u32[]{:S(2)}, u32[]{:S(2)}) async-start(bf16[64,32,128]{2,1,0:T(8,128)(2,1)} %bitcast.6), calls=%async_computation.2 | async-start | bytes 1048576 | tf_op jit(solution)/shard_map/all_to_all | solution.py:56
  72.9 25.3 %copy-start.5 = (s32[16,4]{0,1:T(4,128)S(1)}, s32[16,4]{0,1:T(4,128)}, u32[]{:S(2)}) copy-start(s32[16,4]{0,1:T(4,128)} %param.15) | copy-start | bytes 772
  72.9 25.4 %copy-start.6 = (s32[16]{0:T(128)S(1)}, s32[16]{0:T(128)}, u32[]{:S(2)}) copy-start(s32[16]{0:T(128)} %param.16) | copy-start | bytes 196
  72.9 21.0 %all-to-all-start = ((bf16[128,8,128]{0,2,1:T(8,128)(2,1)}), bf16[128,8,128]{0,2,1:T(8,128)(2,1)S(1)}, u32[]{:S(2)}, u32[]{:S(2)}) async-start(bf16[128,8,128]{0,2,1:T(8,128)(2,1)} %bitcast.1), calls=%async_computation | async-start | bytes 524288 | tf_op jit(solution)/shard_map/all_to_all | solution.py:54
  93.9 10.7 %all-to-all-start.3 = ((bf16[128,8,128]{0,2,1:T(8,128)(2,1)}), bf16[128,8,128]{0,2,1:T(8,128)(2,1)S(1)}, u32[]{:S(2)}, u32[]{:S(2)}) async-start(bf16[128,8,128]{0,2,1:T(8,128)(2,1)} %bitcast.7), calls=%async_computation.3 | async-start | bytes 524288 | tf_op jit(solution)/shard_map/all_to_all | solution.py:53
  197.6 19.1 %copy-start.2 = (bf16[256,1024]{0,1:T(8,128)(2,1)S(1)}, bf16[256,1024]{0,1:T(8,128)(2,1)}, u32[]{:S(2)}) copy-start(bf16[256,1024]{0,1:T(8,128)(2,1)} %copy-done.1) | copy-start | bytes 1572868
  215.1 1.8 copy-start.4
  216.7 0.7 copy-start.7
Sparse Core Ops, SparseCore 0:
  9.5 40.6 all-gather.2
  52.2 38.7 all-gather.4
where the time goes:
time: 226 us; the launch traced here: 225 us
  blocking collectives  78.4 us (35%)
  waiting for transfers between devices  41.5 us (18%)
  local copies, waits for them, and re-layouts  33.7 us (15%)
  matrix products  29.3 us (13%)
  starting transfers between devices  27.1 us (12%)
  between operations  13.5 us (6%)
    all_to_all x1, blocking collectives, body(): lax.all_to_all(attended, 'wide', split_axis=0, concat_axis=0, tiled=True)  43.2 us
    all_to_all x1, waiting for transfers between devices, body(): lax.all_to_all(lax.all_to_all(panel_query, 'grp', split_axis=1, concat_ax...  19.9 us
    all_to_all x1, blocking collectives, body(): lax.all_to_all(panel_query, 'grp', split_axis=1, concat_axis=0, tiled=True)  18.6 us
    all_to_all x1, blocking collectives, body(): lax.all_to_all(lax.all_to_all(attended, 'wide', split_axis=0, concat_axis...  16.5 us
    all_to_all x1, starting transfers between devices, body(): lax.all_to_all(lax.all_to_all(panel_query, 'grp', split_axis=1, concat_ax...  14.8 us
    sub x4, matrix products, softmax_rows(): expo = jnp.exp(scores - top)  12.3 us
    dot_general x4, matrix products, attend(): jnp.einsum('bhij,bjhd->bihd', weights, picked_values, preferred_element_t...  11.7 us
    gather x4, local copies, waits for them, and re-layouts, attend(): key_blocks[listed].reshape(per_step, LMAX * BLK, local_heads, HD)  10.6 us
  transfers between devices with their start and end apart: 5, of which 4 were waited for; matrix products, arithmetic and copies ran while one was open for 5% of the time, Pallas kernels for 0%

commit v1 on v0

--- a/solution.py
+++ b/solution.py
@@ -40,7 +40,9 @@
     flux_weight,
 ):
     full_keys_w, full_values_w = (
-        lax.all_gather(key_weight, "grp", axis=1, tiled=True),
+        jnp.concatenate(
+            lax.all_to_all(jnp.stack([key_weight] * lax.axis_size("grp")), "grp", 0, 0), axis=1
+        ),
         lax.all_gather(value_weight, "grp", axis=1, tiled=True),
     )
     local_keys = jnp.dot(anchor_states, full_keys_w, preferred_element_type=jnp.float32).astype(

time: 226 us -> 245 us (1.084)
  blocking collectives: 78.4 us -> 50.9 us
  waiting for transfers between devices: 41.5 us -> 67 us
  starting transfers between devices: 27.1 us -> 42.6 us
  local copies, waits for them, and re-layouts: 33.7 us -> 39.2 us
    all_to_all x0 -> x2, waiting for transfers between devices: none -> 31.8 us  [the longest x1 25.5 us: body(): lax.all_to_all(jnp.stack([key_weight] * lax.axis_size('grp')), 'grp', 0, 0)]
    all_to_all x1 -> x0, blocking collectives: 18.6 us -> none  [body(): lax.all_to_all(panel_query, 'grp', split_axis=1, concat_axis=0, tiled=True)]
    all_to_all x0 -> x2, starting transfers between devices: none -> 16.2 us  [the longest x1 10.4 us: body(): lax.all_to_all(jnp.stack([key_weight] * lax.axis_size('grp')), 'grp', 0, 0)]
    all_gather x1 -> x0, waiting for transfers between devices: 10.1 us -> none  [body(): lax.all_gather(key_weight, 'grp', axis=1, tiled=True)]
    all_to_all x1, blocking collectives: 43.2 us -> 34.5 us  [body(): lax.all_to_all(attended, 'wide', split_axis=0, concat_axis=0, tiled=True)]
    all_gather x1, waiting for transfers between devices: 6.39 us -> 0.02 us  [body(): lax.all_gather(value_weight, 'grp', axis=1, tiled=True)]
    all_to_all x1, waiting for transfers between devices: 19.9 us -> 26.2 us  [body(): lax.all_to_all(lax.all_to_all(panel_query, 'grp', split_axis=1, concat_ax...]
    all_to_all x1, waiting for transfers between devices: 0.01 us -> 3.78 us  [body(): lax.all_to_all(local_values, 'grp', split_axis=1, concat_axis=0, tiled=True)]
  transfers between devices with their start and end apart: 5 -> 6, of which waited for: 4 -> 5; matrix products, arithmetic and copies ran while one was open for 5% -> 5% of each run, Pallas kernels for 0% -> 0%
where the time goes in v1:
time: 245 us; the launch traced here: 244 us
  waiting for transfers between devices  67 us (27%)
  blocking collectives  50.9 us (21%)
  starting transfers between devices  42.6 us (17%)
  local copies, waits for them, and re-layouts  39.2 us (16%)
  matrix products  28.8 us (12%)
  between operations  13.5 us (6%)
    all_to_all x1, blocking collectives, body(): lax.all_to_all(attended, 'wide', split_axis=0, concat_axis=0, tiled=True)  34.5 us
    all_to_all x1, waiting for transfers between devices, body(): lax.all_to_all(lax.all_to_all(panel_query, 'grp', split_axis=1, concat_ax...  26.2 us
    all_to_all x1, waiting for transfers between devices, body(): lax.all_to_all(jnp.stack([key_weight] * lax.axis_size('grp')), 'grp', 0, 0)  25.5 us
    all_to_all x1, blocking collectives, body(): lax.all_to_all(lax.all_to_all(attended, 'wide', split_axis=0, concat_axis...  16.4 us
    all_to_all x1, starting transfers between devices, body(): lax.all_to_all(lax.all_to_all(panel_query, 'grp', split_axis=1, concat_ax...  12.7 us
    sub x4, matrix products, softmax_rows(): expo = jnp.exp(scores - top)  12.3 us
    dot_general x4, matrix products, attend(): jnp.einsum('bhij,bjhd->bihd', weights, picked_values, preferred_element_t...  11.7 us
    gather x4, local copies, waits for them, and re-layouts, attend(): key_blocks[listed].reshape(per_step, LMAX * BLK, local_heads, HD)  10.6 us
  transfers between devices with their start and end apart: 6, of which 5 were waited for; matrix products, arithmetic and copies ran while one was open for 5% of the time, Pallas kernels for 0%

profile of v1, /device:TPU:1, one launch (start us, length us, event | category | flops | bytes accessed | tf_op | source)
XLA Modules:
  0.0 244.0 jit_solution(16383794095079255475)
XLA Ops:
  9.3 10.4 %all-to-all-start.3 = ((bf16[8,1024,128]{1,2,0:T(8,128)(2,1)}), bf16[8,1024,128]{1,2,0:T(8,128)(2,1)S(1)}, u32[]{:S(2)}, u32[]{:S(2)}) async-start(bf16[8,1024,128]{1,2,0:T(8,128)(2,1)} %stack.2), calls=%async_computation.3 | async-start | bytes 4194304 | tf_op jit(solution)/shard_map/all_to_all | solution.py:44
  20.4 2.0 copy.27
  22.4 25.5 %all-to-all-done.3 = bf16[8,1024,128]{1,2,0:T(8,128)(2,1)S(1)} async-done(((bf16[8,1024,128]{1,2,0:T(8,128)(2,1)}), bf16[8,1024,128]{1,2,0:T(8,128)(2,1)S(1)}, u32[]{:S(2)}, u32[]{:S(2)}) %all-to-all-start.3) | async-done | bytes 2097184 | tf_op jit(solution)/shard_map/all_to_all | solution.py:44
  48.0 5.8 %all-to-all-start.1 = ((bf16[256,8,128]{0,2,1:T(8,128)(2,1)}), bf16[256,8,128]{0,2,1:T(8,128)(2,1)}, u32[]{:S(2)}, u32[]{:S(2)}) async-start(bf16[256,8,128]{0,2,1:T(8,128)(2,1)} %bitcast.82), calls=%async_computation.1 | async-start | bytes 1048576 | tf_op jit(solution)/shard_map/all_to_all | solution.py:59
  57.1 6.3 %all-to-all-done.1 = bf16[256,8,128]{0,2,1:T(8,128)(2,1)} async-done(((bf16[256,8,128]{0,2,1:T(8,128)(2,1)}), bf16[256,8,128]{0,2,1:T(8,128)(2,1)}, u32[]{:S(2)}, u32[]{:S(2)}) %all-to-all-start.1) | async-done | bytes 524320 | tf_op jit(solution)/shard_map/all_to_all | solution.py:59
  63.3 5.9 %all-to-all-start.4 = ((bf16[128,8,128]{0,2,1:T(8,128)(2,1)}), bf16[128,8,128]{0,2,1:T(8,128)(2,1)S(1)}, u32[]{:S(2)}, u32[]{:S(2)}) async-start(bf16[128,8,128]{0,2,1:T(8,128)(2,1)} %bitcast.9), calls=%async_computation.4 | async-start | bytes 524288 | tf_op jit(solution)/shard_map/all_to_all | solution.py:55
  69.2 2.1 copy.30
  71.3 4.5 %all-to-all-done.4 = bf16[128,8,128]{0,2,1:T(8,128)(2,1)S(1)} async-done(((bf16[128,8,128]{0,2,1:T(8,128)(2,1)}), bf16[128,8,128]{0,2,1:T(8,128)(2,1)S(1)}, u32[]{:S(2)}, u32[]{:S(2)}) %all-to-all-start.4) | async-done | bytes 262176 | tf_op jit(solution)/shard_map/all_to_all | solution.py:55
  75.7 12.7 %all-to-all-start.2 = ((bf16[64,32,128]{2,1,0:T(8,128)(2,1)}), bf16[64,32,128]{2,1,0:T(8,128)(2,1)S(1)}, u32[]{:S(2)}, u32[]{:S(2)}) async-start(bf16[64,32,128]{2,1,0:T(8,128)(2,1)} %bitcast.6), calls=%async_computation.2 | async-start | bytes 1048576 | tf_op jit(solution)/shard_map/all_to_all | solution.py:58
  91.3 26.2 %all-to-all-done.2 = bf16[64,32,128]{2,1,0:T(8,128)(2,1)S(1)} async-done(((bf16[64,32,128]{2,1,0:T(8,128)(2,1)}), bf16[64,32,128]{2,1,0:T(8,128)(2,1)S(1)}, u32[]{:S(2)}, u32[]{:S(2)}) %all-to-all-start.2) | async-done | bytes 524320 | tf_op jit(solution)/shard_map/all_to_all | solution.py:58
  117.5 7.9 %all-to-all-start = ((bf16[128,8,128]{0,2,1:T(8,128)(2,1)}), bf16[128,8,128]{0,2,1:T(8,128)(2,1)S(1)}, u32[]{:S(2)}, u32[]{:S(2)}) async-start(bf16[128,8,128]{0,2,1:T(8,128)(2,1)} %bitcast.1), calls=%async_computation | async-start | bytes 524288 | tf_op jit(solution)/shard_map/all_to_all | solution.py:56
  128.2 3.8 %all-to-all-done = bf16[128,8,128]{0,2,1:T(8,128)(2,1)S(1)} async-done(((bf16[128,8,128]{0,2,1:T(8,128)(2,1)}), bf16[128,8,128]{0,2,1:T(8,128)(2,1)S(1)}, u32[]{:S(2)}, u32[]{:S(2)}) %all-to-all-start) | async-done | bytes 262176 | tf_op jit(solution)/shard_map/all_to_all | solution.py:56
  132.4 46.4 %while.11 = (s32[]{:T(128)}, bf16[4,4,128,2,64]{2,4,3,1,0:T(8,128)(2,1)}, s32[4,4,4]{2,1,0:T(4,128)S(1)}, bf16[8,128,2,64]{3,2,1,0:T(2,128)(2,1)S(1)}, s32[4,4]{...) while((s32[]{:T(128)}, ...), condition=%wide.region_3.4_spmd.clone, body=%wide.region_0.3_spmd.clone.sunk | while | flops 137430592 | bytes 7624301 | solution.py:92
  132.5 2.7 %gather_fusion.1 = bf16[16,128,2,64]{3,2,1,0:T(2,128)(2,1)S(1)} fusion(bf16[8,128,2,64]{3,2,1,0:T(2,128)(2,1)S(1)} %get-tuple-element.170, s32[1024]{0:T(1024)S(1)} %pad_clamp_fusion.2), kind=kCustom, calls=%fused_computation.1.clone.clone.1 | custom fusion | bytes 1048640 | tf_op jit(solution)/shard_map/while/body/eval_jaxpr/gather | solution.py:80
  135.4 3.1 %fusion.69 = (f32[4,2,128]{2,1,0:T(2,128)S(1)}, f32[4,2,128,512]{3,2,1,0:T(8,128)}) fusion(pred[4,512]{1,0:T(4,128)(4,1)S(1)} %bitcast.86, bf16[4,512,2,64]{3,2,1,0:T(2,128)(2,1)S(1)} %bitcast.79, bf16[4,4,128,2,64]{2,4,3,1,0:T(8,128)(2,1)} %get-tuple-element.169, s32[]{:T(128)} %get-tuple-element.156), kind=kOutput, calls=%fused_computation.51.clone.1 | convolution fusion | flops 69206528 | bytes 2759168 | tf_op jit(solution)/shard_map/while/body/eval_jaxpr/sub | solution.py:15
  138.4 2.7 %gather_fusion = bf16[16,128,2,64]{3,2,1,0:T(2,128)(2,1)S(1)} fusion(bf16[8,128,2,64]{3,2,1,0:T(2,128)(2,1)S(1)} %get-tuple-element.167, s32[1024]{0:T(1024)S(1)} %pad_clamp_fusion.2), kind=kCustom, calls=%fused_computation.clone.clone.1 | custom fusion | bytes 1048640 | tf_op jit(solution)/shard_map/while/body/eval_jaxpr/gather | solution.py:81
  141.1 2.9 %fusion.70 = bf16[4,4,128,2,64]{2,4,3,1,0:T(8,128)(2,1)} fusion(bf16[4,4,128,2,64]{2,4,3,1,0:T(8,128)(2,1)} %get-tuple-element.157, s32[]{:T(128)} %get-tuple-element.156, bf16[4,512,2,64]{3,2,1,0:T(2,128)(2,1)S(1)} %bitcast.80, f32[4,2,128,512]{3,2,1,0:T(8,128)} %get-tuple-element.146, f32[4,2,128]{2,1,0:T(2,128)S(1)} %get-tuple-element.147), kind=kOutput, calls=%fused_computation.10.clone.1 | convolution fusion | flops 68222976 | bytes 2757120 | tf_op jit(solution)/shard_map/while/body/eval_jaxpr/bhij,bjhd->bihd/dot_general | solution.py:87
  144.1 2.7 %gather_fusion.1 = bf16[16,128,2,64]{3,2,1,0:T(2,128)(2,1)S(1)} fusion(bf16[8,128,2,64]{3,2,1,0:T(2,128)(2,1)S(1)} %get-tuple-element.170, s32[1024]{0:T(1024)S(1)} %pad_clamp_fusion.2), kind=kCustom, calls=%fused_computation.1.clone.clone.1 | custom fusion | bytes 1048640 | tf_op jit(solution)/shard_map/while/body/eval_jaxpr/gather | solution.py:80
  146.9 3.1 %fusion.69 = (f32[4,2,128]{2,1,0:T(2,128)S(1)}, f32[4,2,128,512]{3,2,1,0:T(8,128)}) fusion(pred[4,512]{1,0:T(4,128)(4,1)S(1)} %bitcast.86, bf16[4,512,2,64]{3,2,1,0:T(2,128)(2,1)S(1)} %bitcast.79, bf16[4,4,128,2,64]{2,4,3,1,0:T(8,128)(2,1)} %get-tuple-element.169, s32[]{:T(128)} %get-tuple-element.156), kind=kOutput, calls=%fused_computation.51.clone.1 | convolution fusion | flops 69206528 | bytes 2759168 | tf_op jit(solution)/shard_map/while/body/eval_jaxpr/sub | solution.py:15
  150.0 2.7 %gather_fusion = bf16[16,128,2,64]{3,2,1,0:T(2,128)(2,1)S(1)} fusion(bf16[8,128,2,64]{3,2,1,0:T(2,128)(2,1)S(1)} %get-tuple-element.167, s32[1024]{0:T(1024)S(1)} %pad_clamp_fusion.2), kind=kCustom, calls=%fused_computation.clone.clone.1 | custom fusion | bytes 1048640 | tf_op jit(solution)/shard_map/while/body/eval_jaxpr/gather | solution.py:81
  152.7 2.9 %fusion.70 = bf16[4,4,128,2,64]{2,4,3,1,0:T(8,128)(2,1)} fusion(bf16[4,4,128,2,64]{2,4,3,1,0:T(8,128)(2,1)} %get-tuple-element.157, s32[]{:T(128)} %get-tuple-element.156, bf16[4,512,2,64]{3,2,1,0:T(2,128)(2,1)S(1)} %bitcast.80, f32[4,2,128,512]{3,2,1,0:T(8,128)} %get-tuple-element.146, f32[4,2,128]{2,1,0:T(2,128)S(1)} %get-tuple-element.147), kind=kOutput, calls=%fused_computation.10.clone.1 | convolution fusion | flops 68222976 | bytes 2757120 | tf_op jit(solution)/shard_map/while/body/eval_jaxpr/bhij,bjhd->bihd/dot_general | solution.py:87
  155.7 2.7 %gather_fusion.1 = bf16[16,128,2,64]{3,2,1,0:T(2,128)(2,1)S(1)} fusion(bf16[8,128,2,64]{3,2,1,0:T(2,128)(2,1)S(1)} %get-tuple-element.170, s32[1024]{0:T(1024)S(1)} %pad_clamp_fusion.2), kind=kCustom, calls=%fused_computation.1.clone.clone.1 | custom fusion | bytes 1048640 | tf_op jit(solution)/shard_map/while/body/eval_jaxpr/gather | solution.py:80
  158.6 3.1 %fusion.69 = (f32[4,2,128]{2,1,0:T(2,128)S(1)}, f32[4,2,128,512]{3,2,1,0:T(8,128)}) fusion(pred[4,512]{1,0:T(4,128)(4,1)S(1)} %bitcast.86, bf16[4,512,2,64]{3,2,1,0:T(2,128)(2,1)S(1)} %bitcast.79, bf16[4,4,128,2,64]{2,4,3,1,0:T(8,128)(2,1)} %get-tuple-element.169, s32[]{:T(128)} %get-tuple-element.156), kind=kOutput, calls=%fused_computation.51.clone.1 | convolution fusion | flops 69206528 | bytes 2759168 | tf_op jit(solution)/shard_map/while/body/eval_jaxpr/sub | solution.py:15
  161.6 2.7 %gather_fusion = bf16[16,128,2,64]{3,2,1,0:T(2,128)(2,1)S(1)} fusion(bf16[8,128,2,64]{3,2,1,0:T(2,128)(2,1)S(1)} %get-tuple-element.167, s32[1024]{0:T(1024)S(1)} %pad_clamp_fusion.2), kind=kCustom, calls=%fused_computation.clone.clone.1 | custom fusion | bytes 1048640 | tf_op jit(solution)/shard_map/while/body/eval_jaxpr/gather | solution.py:81
  164.3 2.9 %fusion.70 = bf16[4,4,128,2,64]{2,4,3,1,0:T(8,128)(2,1)} fusion(bf16[4,4,128,2,64]{2,4,3,1,0:T(8,128)(2,1)} %get-tuple-element.157, s32[]{:T(128)} %get-tuple-element.156, bf16[4,512,2,64]{3,2,1,0:T(2,128)(2,1)S(1)} %bitcast.80, f32[4,2,128,512]{3,2,1,0:T(8,128)} %get-tuple-element.146, f32[4,2,128]{2,1,0:T(2,128)S(1)} %get-tuple-element.147), kind=kOutput, calls=%fused_computation.10.clone.1 | convolution fusion | flops 68222976 | bytes 2757120 | tf_op jit(solution)/shard_map/while/body/eval_jaxpr/bhij,bjhd->bihd/dot_general | solution.py:87
  167.3 2.7 %gather_fusion.1 = bf16[16,128,2,64]{3,2,1,0:T(2,128)(2,1)S(1)} fusion(bf16[8,128,2,64]{3,2,1,0:T(2,128)(2,1)S(1)} %get-tuple-element.170, s32[1024]{0:T(1024)S(1)} %pad_clamp_fusion.2), kind=kCustom, calls=%fused_computation.1.clone.clone.1 | custom fusion | bytes 1048640 | tf_op jit(solution)/shard_map/while/body/eval_jaxpr/gather | solution.py:80
  170.2 3.1 %fusion.69 = (f32[4,2,128]{2,1,0:T(2,128)S(1)}, f32[4,2,128,512]{3,2,1,0:T(8,128)}) fusion(pred[4,512]{1,0:T(4,128)(4,1)S(1)} %bitcast.86, bf16[4,512,2,64]{3,2,1,0:T(2,128)(2,1)S(1)} %bitcast.79, bf16[4,4,128,2,64]{2,4,3,1,0:T(8,128)(2,1)} %get-tuple-element.169, s32[]{:T(128)} %get-tuple-element.156), kind=kOutput, calls=%fused_computation.51.clone.1 | convolution fusion | flops 69206528 | bytes 2759168 | tf_op jit(solution)/shard_map/while/body/eval_jaxpr/sub | solution.py:15
  173.2 2.7 %gather_fusion = bf16[16,128,2,64]{3,2,1,0:T(2,128)(2,1)S(1)} fusion(bf16[8,128,2,64]{3,2,1,0:T(2,128)(2,1)S(1)} %get-tuple-element.167, s32[1024]{0:T(1024)S(1)} %pad_clamp_fusion.2), kind=kCustom, calls=%fused_computation.clone.clone.1 | custom fusion | bytes 1048640 | tf_op jit(solution)/shard_map/while/body/eval_jaxpr/gather | solution.py:81
  175.9 2.9 %fusion.70 = bf16[4,4,128,2,64]{2,4,3,1,0:T(8,128)(2,1)} fusion(bf16[4,4,128,2,64]{2,4,3,1,0:T(8,128)(2,1)} %get-tuple-element.157, s32[]{:T(128)} %get-tuple-element.156, bf16[4,512,2,64]{3,2,1,0:T(2,128)(2,1)S(1)} %bitcast.80, f32[4,2,128,512]{3,2,1,0:T(8,128)} %get-tuple-element.146, f32[4,2,128]{2,1,0:T(2,128)S(1)} %get-tuple-element.147), kind=kOutput, calls=%fused_computation.10.clone.1 | convolution fusion | flops 68222976 | bytes 2757120 | tf_op jit(solution)/shard_map/while/body/eval_jaxpr/bhij,bjhd->bihd/dot_general | solution.py:87
  178.8 2.4 copy.37
  181.7 34.5 %all_to_all.84 = bf16[64,32,128]{2,1,0:T(8,128)(2,1)S(1)} all-to-all(bf16[64,32,128]{2,1,0:T(8,128)(2,1)S(1)} %all_to_all.73), channel_id=1, replica_groups=mesh['grp'=8,'wide'=64] {'wide'}, dimensions={0} | all-to-all | bytes 1048576 | tf_op jit(solution)/shard_map/all_to_all | solution.py:95
  216.2 16.4 %all_to_all.85 = bf16[8,256,128]{2,1,0:T(8,128)(2,1)S(1)} all-to-all(bf16[8,256,128]{2,1,0:T(8,128)(2,1)S(1)} %bitcast.83), channel_id=1, replica_groups=mesh['grp'=8,'wide'=64] {'grp'}, dimensions={0} | all-to-all | bytes 1048576 | tf_op jit(solution)/shard_map/all_to_all | solution.py:94
  (65 shorter events, 18.9 us)
Async XLA Ops:
  6.5 229.1 %copy-start = (bf16[1024,512]{1,0:T(8,128)(2,1)S(1)}, bf16[1024,512]{1,0:T(8,128)(2,1)}, u32[]{:S(2)}) copy-start(bf16[1024,512]{1,0:T(8,128)(2,1)} %param.18) | copy-start | bytes 3145732
  9.3 38.7 %all-to-all-start.3 = ((bf16[8,1024,128]{1,2,0:T(8,128)(2,1)}), bf16[8,1024,128]{1,2,0:T(8,128)(2,1)S(1)}, u32[]{:S(2)}, u32[]{:S(2)}) async-start(bf16[8,1024,128]{1,2,0:T(8,128)(2,1)} %stack.2), calls=%async_computation.3 | async-start | bytes 4194304 | tf_op jit(solution)/shard_map/all_to_all | solution.py:44
  19.7 34.1 %copy-start.2 = (bf16[128,1024]{1,0:T(8,128)(2,1)S(1)}, bf16[128,1024]{1,0:T(8,128)(2,1)}, u32[]{:S(2)}) copy-start(bf16[128,1024]{1,0:T(8,128)(2,1)} %param.11) | copy-start | bytes 786436
  19.7 68.8 %all-gather.2.cloned.1.call-start = ((), (), s32[]{:S(2)}) async-start(), calls=%async_computation.7 | async-start | bytes 2359296 | tf_op jit(solution)/shard_map/all_gather | solution.py:46
  48.0 15.4 %all-to-all-start.1 = ((bf16[256,8,128]{0,2,1:T(8,128)(2,1)}), bf16[256,8,128]{0,2,1:T(8,128)(2,1)}, u32[]{:S(2)}, u32[]{:S(2)}) async-start(bf16[256,8,128]{0,2,1:T(8,128)(2,1)} %bitcast.82), calls=%async_computation.1 | async-start | bytes 1048576 | tf_op jit(solution)/shard_map/all_to_all | solution.py:59
  63.3 12.4 %all-to-all-start.4 = ((bf16[128,8,128]{0,2,1:T(8,128)(2,1)}), bf16[128,8,128]{0,2,1:T(8,128)(2,1)S(1)}, u32[]{:S(2)}, u32[]{:S(2)}) async-start(bf16[128,8,128]{0,2,1:T(8,128)(2,1)} %bitcast.9), calls=%async_computation.4 | async-start | bytes 524288 | tf_op jit(solution)/shard_map/all_to_all | solution.py:55
  75.7 41.8 %all-to-all-start.2 = ((bf16[64,32,128]{2,1,0:T(8,128)(2,1)}), bf16[64,32,128]{2,1,0:T(8,128)(2,1)S(1)}, u32[]{:S(2)}, u32[]{:S(2)}) async-start(bf16[64,32,128]{2,1,0:T(8,128)(2,1)} %bitcast.6), calls=%async_computation.2 | async-start | bytes 1048576 | tf_op jit(solution)/shard_map/all_to_all | solution.py:58
  88.4 37.1 %copy-start.4 = (s32[16,4]{0,1:T(4,128)S(1)}, s32[16,4]{0,1:T(4,128)}, u32[]{:S(2)}) copy-start(s32[16,4]{0,1:T(4,128)} %param.15) | copy-start | bytes 772
  88.4 37.2 %copy-start.5 = (s32[16]{0:T(128)S(1)}, s32[16]{0:T(128)}, u32[]{:S(2)}) copy-start(s32[16]{0:T(128)} %param.16) | copy-start | bytes 196
  117.5 14.5 %all-to-all-start = ((bf16[128,8,128]{0,2,1:T(8,128)(2,1)}), bf16[128,8,128]{0,2,1:T(8,128)(2,1)S(1)}, u32[]{:S(2)}, u32[]{:S(2)}) async-start(bf16[128,8,128]{0,2,1:T(8,128)(2,1)} %bitcast.1), calls=%async_computation | async-start | bytes 524288 | tf_op jit(solution)/shard_map/all_to_all | solution.py:56
  232.5 2.6 %copy-start.1 = (bf16[256,1024]{0,1:T(8,128)(2,1)S(1)}, bf16[256,1024]{0,1:T(8,128)(2,1)}, u32[]{:S(2)}) copy-start(bf16[256,1024]{0,1:T(8,128)(2,1)} %copy.27) | copy-start | bytes 1572868
  233.6 1.8 copy-start.3
  235.2 0.7 copy-start.6
Sparse Core Ops, SparseCore 0:
  22.6 41.3 all-gather.1
